TPU v7x, 32 devices: a whole 2x2x4 slice. The times are simulated.
32 devices in a mesh: dom: 8 (over y, x, core), sub: 4 (over z).
Axes of the slice: x: 2, y: 2, z: 4, core: 2. Of those that a mesh axis runs over, the one named last changes fastest.
Arguments:
- adjoint_rhs: float32 [384, 320], P(('dom', 'sub')), may hold values from -6 to 6
- adjoint_start: float32 [384, 320], P(('dom', 'sub')), may hold values from -6 to 6
- offdiag_blocks: bfloat16 [6, 384, 320, 320], P(None, ('dom', 'sub')), may hold values from -0.125 to 0.125
- diag_inverse: float32 [384, 320, 320], P(('dom', 'sub')), may hold values from -0.3125 to 0.3125
- geometry_jac: bfloat16 [384, 24, 320], P(('dom', 'sub')), may hold values from -0.125 to 0.125
- neighbor: int32 [384, 6], P(('dom', 'sub')), may hold values from -1 to 383, as said below
- corner_node: int32 [384, 8], P(('dom', 'sub')), may hold values from 0 to 566, as said below
- deform_place: int32 [567], replicated, may hold values from 0 to 575, as said below
- stiff_diag: float32 [3, 3, 576], P(None, None, ('dom', 'sub')), may hold values from -3.5 to 3.5
- stiff_upper: float32 [3, 3, 576], P(None, None, ('dom', 'sub')), may hold values from -3.5 to 3.5
- stiff_lower: float32 [3, 3, 576], P(None, None, ('dom', 'sub')), may hold values from -3.5 to 3.5
Outputs:
- adjoint: float32 [384, 320], P(('dom', 'sub'))
- shape_grad: float32 [3, 576], P(None, ('dom', 'sub'))
Inputs may be any that keep to these rules, and one draw needn't show every extreme that they name: Elements are numbered device by device in the order of dom then sub, 12 to a device. The relation is symmetric: neighbor[e, k] = f >= 0 implies neighbor[f, k xor 1] = e. A neighbour across face 0 or 1 lies on the same device or on the device one step up (face 0) or down (face 1) along dom with the same sub index; across face 2 or 3 on the same device or one step up (face 2) or down (face 3) along sub; across faces 4 and 5 on the same device. At most 12 faces 0 of one device, and as many faces 1, lead to another device, and at most 6 faces 2, and as many faces 3; these counts are reached. `corner_node`: elements that share a corner name the same node. `deform_place`: the positions are distinct.
All inputs are finite; a program needn't handle non-finite values.
Results may differ from a plain program's by a relative error of at most 0.0042.
Values sent between devices are 32-bit elements; how exact they have to be, the bound alone decides.
No kernel may reach another device: no remote copies, remote signals or barrier semaphores. Data moves between devices by JAX's collectives and lax.ppermute only.
A program may use at most 128 MiB of HBM per device.

v0:
```python
import jax
import jax.numpy as jnp
from jax import lax
from jax.sharding import PartitionSpec as P

NF = 6
BX = 1
BY = 2
BZ = 6
SWEEPS = 2
precise = lax.Precision.HIGHEST


def passed_along(value, axis, steps):
    count = lax.axis_size(axis)
    initial, last = (max(0, -steps), min(count, count - steps))
    return lax.ppermute(value, axis, [(source, source + steps) for source in range(initial, last)])


def padded_2(block, sides, width):
    for axis, dim in sides:
        count = lax.axis_size(axis)
        forward = [(i, i + 1) for i in range(count - 1)]
        backward = [(target, source) for source, target in forward]
        low = lax.ppermute(
            lax.slice_in_dim(block, block.shape[dim] - width, None, axis=dim), axis, forward
        )
        high = lax.ppermute(lax.slice_in_dim(block, 0, width, axis=dim), axis, backward)
        block = jnp.concatenate([low, block, high], axis=dim)
    return block


def dom_move(packed, offset):
    return passed_along(packed, "dom", offset)


def sub_move(packed, offset):
    return passed_along(packed, "sub", offset)


def slot_tables(neighbor, remote, capacity, face_index):
    face_ids = neighbor[:, face_index]
    chosen = remote[:, face_index]
    earlier = chosen[None, :] & (face_ids[None, :] < face_ids[:, None])
    send_rank = jnp.sum(earlier.astype(jnp.int32), 1)
    slot_range = jnp.arange(capacity, dtype=jnp.int32)
    send_table = (chosen[:, None] & (send_rank[:, None] == slot_range[None, :])).astype(jnp.float32)
    receive_rank = jnp.cumsum(chosen.astype(jnp.int32)) - 1
    receive_table = (chosen[:, None] & (receive_rank[:, None] == slot_range[None, :])).astype(
        jnp.float32
    )
    return (send_table, receive_table)


def on_device(
    adjoint_rhs,
    adjoint_start,
    offdiag_blocks,
    diag_inverse,
    geometry_jac,
    neighbor,
    corner_node,
    deform_place,
    stiff_diag,
    stiff_upper,
    stiff_lower,
):
    elem_count = adjoint_rhs.shape[0]
    block_size = adjoint_rhs.shape[1]
    device = lax.axis_index(("dom", "sub"))
    first_id = device * elem_count
    has_face = neighbor >= 0
    inside = has_face & (neighbor >= first_id) & (neighbor < first_id + elem_count)
    remote = has_face & jnp.logical_not(inside)
    target = jnp.where(inside, neighbor - first_id, elem_count)
    columns = jnp.arange(elem_count, dtype=jnp.int32)
    local_map = (
        (target.T[:, :, None] == columns[None, None, :])
        .astype(jnp.float32)
        .reshape(NF * elem_count, elem_count)
    )
    tables = [
        slot_tables(neighbor, remote, BY * BZ, 0),
        slot_tables(neighbor, remote, BY * BZ, 1),
        slot_tables(neighbor, remote, BX * BZ, 2),
        slot_tables(neighbor, remote, BX * BZ, 3),
    ]
    adjoint = adjoint_start
    for sweep_index in range(SWEEPS):
        rounded = adjoint.astype(jnp.bfloat16)
        face_terms = jnp.einsum(
            "keij,ei->kej", offdiag_blocks, rounded, preferred_element_type=jnp.float32
        )
        stacked_terms = face_terms.reshape(NF * elem_count, block_size)
        carried = jnp.dot(local_map.T, stacked_terms, precision=precise)
        for face_index in range(4):
            packed = jnp.dot(tables[face_index][0].T, face_terms[face_index], precision=precise)
            if face_index < 2:
                arrived = dom_move(packed, 1 - 2 * face_index)
            else:
                arrived = sub_move(packed, 5 - 2 * face_index)
            carried = carried + jnp.dot(tables[face_index ^ 1][1], arrived, precision=precise)
        adjoint = jnp.einsum("eij,ej->ei", diag_inverse, adjoint_rhs - carried, precision=precise)
    rounded = adjoint.astype(jnp.bfloat16)
    corner_terms = jnp.einsum(
        "emi,ei->em", geometry_jac, rounded, preferred_element_type=jnp.float32
    )
    values = corner_terms.reshape(elem_count, 8, 3).transpose(2, 0, 1).reshape(3, 8 * elem_count)
    places = deform_place[corner_node.reshape(-1)]
    node_count = stiff_diag.shape[2]
    every_value = lax.all_gather(values, ("dom", "sub"), axis=1, tiled=True)
    every_place = lax.all_gather(places, ("dom", "sub"), axis=0, tiled=True)
    node_slot = every_place - device * node_count
    owned = (node_slot >= 0) & (node_slot < node_count)
    node_slot = jnp.where(owned, node_slot, node_count)
    node_sens = jax.ops.segment_sum(every_value.T, node_slot, node_count + 1)[:node_count].T
    upper_term = jnp.einsum("abq,aq->bq", stiff_upper, node_sens, precision=precise)
    stacked = jnp.concatenate([upper_term, node_sens], 0)
    padded = padded_2(stacked, ((("dom", "sub"), 1),), 1)
    shape_grad = (
        jnp.einsum("abq,aq->bq", stiff_diag, node_sens, precision=precise) + padded[0:3, :-2]
    )
    shape_grad = shape_grad + jnp.einsum(
        "abq,aq->bq", stiff_lower, padded[3:6, 2:], precision=precise
    )
    return (adjoint, shape_grad)


def solution(mesh):
    placed = (
        P(("dom", "sub"), None),
        P(("dom", "sub"), None),
        P(None, ("dom", "sub"), None, None),
        P(("dom", "sub"), None, None),
        P(("dom", "sub"), None, None),
        P(("dom", "sub"), None),
        P(("dom", "sub"), None),
        P(),
        P(None, None, ("dom", "sub")),
        P(None, None, ("dom", "sub")),
        P(None, None, ("dom", "sub")),
    )
    return jax.shard_map(
        on_device,
        mesh=mesh,
        in_specs=placed,
        out_specs=(P(("dom", "sub"), None), P(None, ("dom", "sub"))),
        check_vma=False,
    )
```

profile of v0, /device:TPU:27, one launch (start us, length us, event | category | flops | bytes accessed | tf_op | source)
XLA Modules:
  0.0 206.3 jit_solution(1495273788116148652)
XLA Ops:
  0.7 0.8 slice_bitcast_fusion.24
  1.5 0.7 not_and_fusion
  2.2 0.7 convert_bitcast_fusion.1
  3.0 8.5 %fusion.2 = f32[12,1,6,320]{3,1,2,0:T(1,128)S(1)} fusion(bf16[6,12,320,320]{3,2,1,0:T(8,128)(2,1)} %param.13, bf16[12,320,1,1]{1,0,2,3:T(8,128)(2,1)S(1)} %convert_bitcast_fusion.1), kind=kOutput, calls=%fused_computation.4 | convolution fusion | flops 14745600 | bytes 14845440 | tf_op jit(solution)/shard_map/keij,ei->kej/dot_general | solution.py:91
  11.6 0.3 fusion.20
  11.9 2.6 %collective-permute-start.1 = (f32[12,320]{1,0:T(8,128)S(1)}, f32[12,320]{1,0:T(8,128)S(1)}, u32[]{:S(2)}, u32[]{:S(2)}) collective-permute-start(f32[12,320]{1,0:T(8,128)S(1)} %fusion.20), channel_id=1, source_target_pairs={{4,0},{8,4},{12,8},{16,12},{20,16},{24,20},{28,24},{5,1},{9,5},{13... | collective-permute-start | bytes 46088 | tf_op jit(solution)/shard_map/ppermute | solution.py:17
  14.7 0.3 fusion.19
  14.9 1.3 collective-permute-start.2
  16.4 0.3 fusion.18
  16.7 4.0 %collective-permute-start.3 = (f32[6,320]{1,0:T(8,128)S(1)}, f32[6,320]{1,0:T(8,128)S(1)}, u32[]{:S(2)}, u32[]{:S(2)}) collective-permute-start(f32[6,320]{1,0:T(8,128)S(1)} %fusion.18), channel_id=1, source_target_pairs={{1,0},{2,1},{3,2},{5,4},{6,5},{7,6},{9,8},{10,9},{11,10},{13,12},{... | collective-permute-start | bytes 23048 | tf_op jit(solution)/shard_map/ppermute | solution.py:17
  20.9 0.3 fusion.21
  21.1 4.4 %collective-permute-start = (f32[12,320]{1,0:T(8,128)S(1)}, f32[12,320]{1,0:T(8,128)S(1)}, u32[]{:S(2)}, u32[]{:S(2)}) collective-permute-start(f32[12,320]{1,0:T(8,128)S(1)} %fusion.21), channel_id=1, source_target_pairs={{0,4},{4,8},{8,12},{12,16},{16,20},{20,24},{24,28},{1,5},{5,9},{9,... | collective-permute-start | bytes 46088 | tf_op jit(solution)/shard_map/ppermute | solution.py:17
  25.6 0.2 reduce-window.33
  25.8 0.2 reduce-window.34
  26.0 0.2 reduce-window.35
  26.6 1.0 gather_fusion
  27.6 0.3 dynamic-update-slice
  27.9 36.6 %all-reduce = s32[3072]{0:T(1024)S(1)} all-reduce(s32[3072]{0:T(1024)S(1)} %dynamic-update-slice), channel_id=2, replica_groups=mesh['dom'=8,'sub'=4] {'dom','sub'}, use_global_device_ids=true, to_apply=%add | all-reduce | flops 3072 | bytes 24576
  64.5 0.2 convolution_bitcast_fusion.1
  64.7 0.2 fusion.50
  64.9 0.2 fusion.58
  65.1 0.2 fusion.42
  65.3 0.2 fusion.13
  65.6 7.5 %fusion.29 = bf16[12,1,320]{2,1,0:T(2,128)(2,1)S(1)} fusion(f32[12,320,320]{2,1,0:T(8,128)} %param.14, f32[12,320,1]{1,0,2:T(8,128)S(1)} %fusion.13), kind=kOutput, calls=%fused_computation.48 | convolution fusion | flops 14745600 | bytes 4938240 | tf_op jit(solution)/shard_map/eij,ej->ei/dot_general | solution.py:103
  73.2 8.6 %fusion = f32[12,1,6,320]{3,1,2,0:T(1,128)S(1)} fusion(bf16[6,12,320,320]{3,2,1,0:T(8,128)(2,1)} %param.13, bf16[12,320,1,1]{1,0,2,3:T(8,128)(2,1)S(1)} %bitcast.130), kind=kOutput, calls=%fused_computation.2 | convolution fusion | flops 14745600 | bytes 14845440 | tf_op jit(solution)/shard_map/keij,ei->kej/dot_general | solution.py:91
  81.7 0.3 fusion.16
  82.0 0.3 fusion.15
  82.3 0.3 fusion.17
  82.5 0.3 fusion.14
  82.8 1.3 collective-permute-start.6
  84.1 0.2 convolution_bitcast_fusion
  84.3 4.4 %collective-permute-start.5 = (f32[12,320]{1,0:T(8,128)S(1)}, f32[12,320]{1,0:T(8,128)S(1)}, u32[]{:S(2)}, u32[]{:S(2)}) collective-permute-start(f32[12,320]{1,0:T(8,128)S(1)} %fusion.16), channel_id=1, source_target_pairs={{4,0},{8,4},{12,8},{16,12},{20,16},{24,20},{28,24},{5,1},{9,5},{13... | collective-permute-start | bytes 46088 | tf_op jit(solution)/shard_map/ppermute | solution.py:17
  88.7 3.0 %collective-permute-start.4 = (f32[12,320]{1,0:T(8,128)S(1)}, f32[12,320]{1,0:T(8,128)S(1)}, u32[]{:S(2)}, u32[]{:S(2)}) collective-permute-start(f32[12,320]{1,0:T(8,128)S(1)} %fusion.17), channel_id=1, source_target_pairs={{0,4},{4,8},{8,12},{12,16},{16,20},{20,24},{24,28},{1,5},{5,9},{9,... | collective-permute-start | bytes 46088 | tf_op jit(solution)/shard_map/ppermute | solution.py:17
  91.8 4.4 %collective-permute-start.7 = (f32[6,320]{1,0:T(8,128)S(1)}, f32[6,320]{1,0:T(8,128)S(1)}, u32[]{:S(2)}, u32[]{:S(2)}) collective-permute-start(f32[6,320]{1,0:T(8,128)S(1)} %fusion.14), channel_id=1, source_target_pairs={{1,0},{2,1},{3,2},{5,4},{6,5},{7,6},{9,8},{10,9},{11,10},{13,12},{... | collective-permute-start | bytes 23048 | tf_op jit(solution)/shard_map/ppermute | solution.py:17
  96.2 0.2 fusion.48
  96.4 0.4 collective-permute-done.7
  96.8 0.2 fusion.56
  97.1 0.2 fusion.40
  97.3 0.2 fusion.8
  97.5 5.2 %fusion.26 = f32[12,1,320]{2,1,0:T(1,128)S(1)} fusion(f32[12,320,320]{2,1,0:T(8,128)S(1)} %bitcast.128, f32[12,320,1]{1,0,2:T(8,128)S(1)} %fusion.8), kind=kOutput, calls=%fused_computation.45 | convolution fusion | flops 14745600 | bytes 4945920 | tf_op jit(solution)/shard_map/eij,ej->ei/dot_general | solution.py:103
  102.7 0.6 convert_bitcast_fusion
  103.8 63.5 %all-gather.1 = f32[32,96,3]{1,2,0:T(4,128)S(1)} all-gather(f32[1,96,3]{1,2,0:T(4,128)S(1)} %bitcast.143), channel_id=1, replica_groups=mesh['dom'=8,'sub'=4] {'dom','sub'}, dimensions={0}, use_global_device_ids=true | all-gather | bytes 38016 | tf_op jit(solution)/shard_map/all_gather | solution.py:111
  167.4 0.5 copy.66
  167.9 21.1 %scatter_custom_fusion = f32[19,3]{1,0:T(8,128)S(1)} fusion(s32[3072]{0:T(1024)S(1)} %and_select_fusion, f32[3072,3]{1,0:T(8,128)S(1)} %bitcast.129, f32[]{:T(128)} %constant.34.clone.1), kind=kCustom, calls=%fused_computation.84 | custom fusion | flops 9216 | bytes 232 | tf_op jit(solution)/shard_map/scatter-add | solution.py:116
  189.3 7.8 %collective-permute-start.8 = (f32[6,1]{1,0:T(8,128)S(1)}, f32[6,1]{1,0:T(8,128)S(1)}, u32[]{:S(2)}, u32[]{:S(2)}) collective-permute-start(f32[6,1]{1,0:T(8,128)S(1)} %get-tuple-element.18), channel_id=1, source_target_pairs={{0,1},{1,2},{2,3},{3,4},{4,5},{5,6},{6,7},{7,8},{8,9},{9,10},{10,1... | collective-permute-start | bytes 80 | tf_op jit(solution)/shard_map/ppermute | solution.py:25
  197.1 1.9 collective-permute-start.9
  199.0 6.6 %collective-permute-done.9 = f32[6,1]{1,0:T(8,128)S(1)} collective-permute-done((f32[6,1]{1,0:T(8,128)S(1)}, f32[6,1]{1,0:T(8,128)S(1)}, u32[]{:S(2)}, u32[]{:S(2)}) %collective-permute-start.9) | collective-permute-done | bytes 56 | tf_op jit(solution)/shard_map/ppermute | solution.py:28
  205.8 0.6 bitcast_add_fusion
  (63 shorter events, 2.2 us)
Async XLA Ops:
  0.6 102.7 %copy-start = (bf16[12,24,320]{2,1,0:T(8,128)(2,1)S(1)}, bf16[12,24,320]{2,1,0:T(8,128)(2,1)}, u32[]{:S(2)}) copy-start(bf16[12,24,320]{2,1,0:T(8,128)(2,1)} %param.15) | copy-start | bytes 552964
  2.9 22.6 %copy-start.3 = (s32[12,6]{0,1:T(8,128)S(1)}, s32[12,6]{0,1:T(8,128)}, u32[]{:S(2)}) copy-start(s32[12,6]{0,1:T(8,128)} %param.16) | copy-start | bytes 868
  2.9 23.4 %copy-start.7 = (s32[12,8]{0,1:T(8,128)S(1)}, s32[12,8]{0,1:T(8,128)}, u32[]{:S(2)}) copy-start(s32[12,8]{0,1:T(8,128)} %param.17) | copy-start | bytes 1156
  2.9 23.6 %copy-start.1 = (s32[567]{0:T(1024)S(1)}, s32[567]{0:T(1024)}, u32[]{:S(2)}) copy-start(s32[567]{0:T(1024)} %param.18) | copy-start | bytes 6808
  3.0 62.4 %copy-start.2 = (f32[12,320]{1,0:T(8,128)S(1)}, f32[12,320]{1,0:T(8,128)}, u32[]{:S(2)}) copy-start(f32[12,320]{1,0:T(8,128)} %param.11) | copy-start | bytes 46084
  11.9 53.2 %collective-permute-start.1 = (f32[12,320]{1,0:T(8,128)S(1)}, f32[12,320]{1,0:T(8,128)S(1)}, u32[]{:S(2)}, u32[]{:S(2)}) collective-permute-start(f32[12,320]{1,0:T(8,128)S(1)} %fusion.20), channel_id=1, source_target_pairs={{4,0},{8,4},{12,8},{16,12},{20,16},{24,20},{28,24},{5,1},{9,5},{13... | collective-permute-start | bytes 46088 | tf_op jit(solution)/shard_map/ppermute | solution.py:17
  14.9 49.7 %collective-permute-start.2 = (f32[6,320]{1,0:T(8,128)S(1)}, f32[6,320]{1,0:T(8,128)S(1)}, u32[]{:S(2)}, u32[]{:S(2)}) collective-permute-start(f32[6,320]{1,0:T(8,128)S(1)} %fusion.19), channel_id=1, source_target_pairs={{0,1},{1,2},{2,3},{4,5},{5,6},{6,7},{8,9},{9,10},{10,11},{12,13},{... | collective-permute-start | bytes 23048 | tf_op jit(solution)/shard_map/ppermute | solution.py:17
  16.7 48.2 %collective-permute-start.3 = (f32[6,320]{1,0:T(8,128)S(1)}, f32[6,320]{1,0:T(8,128)S(1)}, u32[]{:S(2)}, u32[]{:S(2)}) collective-permute-start(f32[6,320]{1,0:T(8,128)S(1)} %fusion.18), channel_id=1, source_target_pairs={{1,0},{2,1},{3,2},{5,4},{6,5},{7,6},{9,8},{10,9},{11,10},{13,12},{... | collective-permute-start | bytes 23048 | tf_op jit(solution)/shard_map/ppermute | solution.py:17
  21.1 44.2 %collective-permute-start = (f32[12,320]{1,0:T(8,128)S(1)}, f32[12,320]{1,0:T(8,128)S(1)}, u32[]{:S(2)}, u32[]{:S(2)}) collective-permute-start(f32[12,320]{1,0:T(8,128)S(1)} %fusion.21), channel_id=1, source_target_pairs={{0,4},{4,8},{8,12},{12,16},{16,20},{20,24},{24,28},{1,5},{5,9},{9,... | collective-permute-start | bytes 46088 | tf_op jit(solution)/shard_map/ppermute | solution.py:17
  65.6 31.9 %slice-start = ((s8[5898240]{0:T(1024)(128)(4,1)}), s8[4194304]{0:T(1024)(128)(4,1)S(1)}, s32[]{:S(2)}) async-start(s8[5898240]{0:T(1024)(128)(4,1)} %bitcast.127), calls=%async_computation | async-start | bytes 8388608
  73.1 24.4 %slice-start.1 = ((s8[5898240]{0:T(1024)(128)(4,1)}), s8[1703936]{0:T(1024)(128)(4,1)S(1)}, s32[]{:S(2)}) async-start(s8[5898240]{0:T(1024)(128)(4,1)} %bitcast.127), calls=%async_computation.1 | async-start | bytes 3407872
  81.7 107.5 %copy-start.5 = (f32[3,3,18]{2,1,0:T(4,128)S(1)}, f32[3,3,18]{2,1,0:T(4,128)}, u32[]{:S(2)}) copy-start(f32[3,3,18]{2,1,0:T(4,128)} %param.19) | copy-start | bytes 1948
  81.7 107.5 %copy-start.6 = (f32[3,3,18]{2,1,0:T(4,128)S(1)}, f32[3,3,18]{2,1,0:T(4,128)}, u32[]{:S(2)}) copy-start(f32[3,3,18]{2,1,0:T(4,128)} %param.20) | copy-start | bytes 1948
  81.7 124.0 %copy-start.4 = (f32[3,3,18]{2,1,0:T(4,128)S(1)}, f32[3,3,18]{2,1,0:T(4,128)}, u32[]{:S(2)}) copy-start(f32[3,3,18]{2,1,0:T(4,128)} %param.21) | copy-start | bytes 1948
  82.8 13.4 %collective-permute-start.6 = (f32[6,320]{1,0:T(8,128)S(1)}, f32[6,320]{1,0:T(8,128)S(1)}, u32[]{:S(2)}, u32[]{:S(2)}) collective-permute-start(f32[6,320]{1,0:T(8,128)S(1)} %fusion.15), channel_id=1, source_target_pairs={{0,1},{1,2},{2,3},{4,5},{5,6},{6,7},{8,9},{9,10},{10,11},{12,13},{... | collective-permute-start | bytes 23048 | tf_op jit(solution)/shard_map/ppermute | solution.py:17
  84.3 12.7 %collective-permute-start.5 = (f32[12,320]{1,0:T(8,128)S(1)}, f32[12,320]{1,0:T(8,128)S(1)}, u32[]{:S(2)}, u32[]{:S(2)}) collective-permute-start(f32[12,320]{1,0:T(8,128)S(1)} %fusion.16), channel_id=1, source_target_pairs={{4,0},{8,4},{12,8},{16,12},{20,16},{24,20},{28,24},{5,1},{9,5},{13... | collective-permute-start | bytes 46088 | tf_op jit(solution)/shard_map/ppermute | solution.py:17
  88.7 8.5 %collective-permute-start.4 = (f32[12,320]{1,0:T(8,128)S(1)}, f32[12,320]{1,0:T(8,128)S(1)}, u32[]{:S(2)}, u32[]{:S(2)}) collective-permute-start(f32[12,320]{1,0:T(8,128)S(1)} %fusion.17), channel_id=1, source_target_pairs={{0,4},{4,8},{8,12},{12,16},{16,20},{20,24},{24,28},{1,5},{5,9},{9,... | collective-permute-start | bytes 46088 | tf_op jit(solution)/shard_map/ppermute | solution.py:17
  91.8 5.1 %collective-permute-start.7 = (f32[6,320]{1,0:T(8,128)S(1)}, f32[6,320]{1,0:T(8,128)S(1)}, u32[]{:S(2)}, u32[]{:S(2)}) collective-permute-start(f32[6,320]{1,0:T(8,128)S(1)} %fusion.14), channel_id=1, source_target_pairs={{1,0},{2,1},{3,2},{5,4},{6,5},{7,6},{9,8},{10,9},{11,10},{13,12},{... | collective-permute-start | bytes 23048 | tf_op jit(solution)/shard_map/ppermute | solution.py:17
  189.3 9.7 %collective-permute-start.8 = (f32[6,1]{1,0:T(8,128)S(1)}, f32[6,1]{1,0:T(8,128)S(1)}, u32[]{:S(2)}, u32[]{:S(2)}) collective-permute-start(f32[6,1]{1,0:T(8,128)S(1)} %get-tuple-element.18), channel_id=1, source_target_pairs={{0,1},{1,2},{2,3},{3,4},{4,5},{5,6},{6,7},{7,8},{8,9},{9,10},{10,1... | collective-permute-start | bytes 80 | tf_op jit(solution)/shard_map/ppermute | solution.py:25
  197.1 8.5 %collective-permute-start.9 = (f32[6,1]{1,0:T(8,128)S(1)}, f32[6,1]{1,0:T(8,128)S(1)}, u32[]{:S(2)}, u32[]{:S(2)}) collective-permute-start(f32[6,1]{1,0:T(8,128)S(1)} %get-tuple-element.19), channel_id=1, source_target_pairs={{1,0},{2,1},{3,2},{4,3},{5,4},{6,5},{7,6},{8,7},{9,8},{10,9},{11,1... | collective-permute-start | bytes 80 | tf_op jit(solution)/shard_map/ppermute | solution.py:28
where the time goes:
time: 207 us; the launch traced here: 206 us
  blocking collectives  100 us (48%)
  starting transfers between devices  35.1 us (17%)
  matrix products  34.2 us (17%)
  other arithmetic  25.4 us (12%)
  waiting for transfers between devices  7.03 us (3%)
  local copies, waits for them, and re-layouts  3.49 us (2%)
    all_gather x1, blocking collectives, on_device(): every_value = lax.all_gather(values, ('dom', 'sub'), axis=1, tiled=True)  63.5 us
    unnamed x1, blocking collectives  36.6 us
    ppermute x8, starting transfers between devices, passed_along(): lax.ppermute(value, axis, [(source, source + steps) for source in range(i...  25.4 us
    scatter-add x1, other arithmetic, on_device(): jax.ops.segment_sum(every_value.T, node_slot, node_count + 1)[:node_count]  21.1 us
    dot_general x2, matrix products, on_device(): jnp.einsum('keij,ei->kej', offdiag_blocks, rounded, preferred_element_typ...  17 us
    dot_general x2, matrix products, on_device(): jnp.einsum('eij,ej->ei', diag_inverse, adjoint_rhs - carried, precision=p...  12.8 us
    ppermute x1, starting transfers between devices, padded_2(): lax.ppermute(lax.slice_in_dim(block, block.shape[dim] - width, None, axis...  7.75 us
    ppermute x1, waiting for transfers between devices, padded_2(): lax.ppermute(lax.slice_in_dim(block, 0, width, axis=dim), axis, backward)  6.58 us
  transfers between devices with their start and end apart: 10, of which 2 were waited for; matrix products, arithmetic and copies ran while one was open for 3% of the time, Pallas kernels for 0%

commit v1 on v0

--- a/solution.py
+++ b/solution.py
@@ -9,6 +9,24 @@
 BZ = 6
 SWEEPS = 2
 precise = lax.Precision.HIGHEST
+
+
+def joined_along(blocks, dim):
+    shape = list(blocks.shape[1:])
+    shape[dim] *= blocks.shape[0]
+    return jnp.moveaxis(blocks, 0, dim).reshape(shape)
+
+
+def collected_by_bits(x, axis):
+    size = lax.axis_size(axis)
+    tiles = x[None]
+    for level in range(size.bit_length() - 1):
+        bit = 1 << level
+        other = lax.ppermute(tiles, axis, [(i, i ^ bit) for i in range(size)])
+        both = jnp.stack([tiles, other])
+        upper = lax.axis_index(axis) >> level & 1
+        tiles = jnp.where(upper == 0, both, both[::-1]).reshape(-1, *x.shape)
+    return tiles
 
 
 def passed_along(value, axis, steps):
@@ -108,7 +126,7 @@
     values = corner_terms.reshape(elem_count, 8, 3).transpose(2, 0, 1).reshape(3, 8 * elem_count)
     places = deform_place[corner_node.reshape(-1)]
     node_count = stiff_diag.shape[2]
-    every_value = lax.all_gather(values, ("dom", "sub"), axis=1, tiled=True)
+    every_value = joined_along(collected_by_bits(values, ("dom", "sub")), 1)
     every_place = lax.all_gather(places, ("dom", "sub"), axis=0, tiled=True)
     node_slot = every_place - device * node_count
     owned = (node_slot >= 0) & (node_slot < node_count)

time: 207 us -> 158 us (0.76)
  blocking collectives: 100 us -> 41.3 us
  starting transfers between devices: 35.1 us -> 40 us
  waiting for transfers between devices: 7.03 us -> 11.8 us
    all_gather x1 -> x0, blocking collectives: 63.5 us -> none  [on_device(): every_value = lax.all_gather(values, ('dom', 'sub'), axis=1, tiled=True)]
    ppermute x0 -> x5, starting transfers between devices: none -> 5.92 us  [collected_by_bits(): other = lax.ppermute(tiles, axis, [(i, i ^ bit) for i in range(size)])]
    ppermute x0 -> x5, waiting for transfers between devices: none -> 4.77 us  [collected_by_bits(): other = lax.ppermute(tiles, axis, [(i, i ^ bit) for i in range(size)])]
    unnamed x1, blocking collectives: 36.6 us -> 41.3 us
  transfers between devices with their start and end apart: 10 -> 15, of which waited for: 2 -> 6; matrix products, arithmetic and copies ran while one was open for 3% -> 3% of each run, Pallas kernels for 0% -> 0%
where the time goes in v1:
time: 158 us; the launch traced here: 157 us
  blocking collectives  41.3 us (26%)
  starting transfers between devices  40 us (25%)
  matrix products  34.1 us (22%)
  other arithmetic  25.5 us (16%)
  waiting for transfers between devices  11.8 us (7%)
  local copies, waits for them, and re-layouts  3.61 us (2%)
    unnamed x1, blocking collectives  41.3 us
    ppermute x8, starting transfers between devices, passed_along(): lax.ppermute(value, axis, [(source, source + steps) for source in range(i...  24.3 us
    scatter-add x1, other arithmetic, on_device(): jax.ops.segment_sum(every_value.T, node_slot, node_count + 1)[:node_count]  21.1 us
    dot_general x2, matrix products, on_device(): jnp.einsum('keij,ei->kej', offdiag_blocks, rounded, preferred_element_typ...  17 us
    dot_general x2, matrix products, on_device(): jnp.einsum('eij,ej->ei', diag_inverse, adjoint_rhs - carried, precision=p...  12.8 us
    ppermute x1, starting transfers between devices, padded_2(): lax.ppermute(lax.slice_in_dim(block, block.shape[dim] - width, None, axis...  7.79 us
    ppermute x1, waiting for transfers between devices, padded_2(): lax.ppermute(lax.slice_in_dim(block, 0, width, axis=dim), axis, backward)  6.58 us
    ppermute x5, starting transfers between devices, collected_by_bits(): other = lax.ppermute(tiles, axis, [(i, i ^ bit) for i in range(size)])  5.92 us
  transfers between devices with their start and end apart: 15, of which 6 were waited for; matrix products, arithmetic and copies ran while one was open for 3% of the time, Pallas kernels for 0%

profile of v1, /device:TPU:27, one launch (start us, length us, event | category | flops | bytes accessed | tf_op | source)
XLA Modules:
  0.0 157.3 jit_solution(4877667678205106190)
XLA Ops:
  0.7 0.8 slice_bitcast_fusion.24
  1.5 0.7 not_and_fusion
  2.2 0.7 convert_bitcast_fusion.1
  2.9 8.4 %fusion.2 = f32[12,1,6,320]{3,1,2,0:T(1,128)S(1)} fusion(bf16[6,12,320,320]{3,2,1,0:T(8,128)(2,1)} %param.13, bf16[12,320,1,1]{1,0,2,3:T(8,128)(2,1)S(1)} %convert_bitcast_fusion.1), kind=kOutput, calls=%fused_computation.4 | convolution fusion | flops 14745600 | bytes 14845440 | tf_op jit(solution)/shard_map/keij,ei->kej/dot_general | solution.py:109
  11.6 0.3 fusion.20
  11.9 2.6 %collective-permute-start.1 = (f32[12,320]{1,0:T(8,128)S(1)}, f32[12,320]{1,0:T(8,128)S(1)}, u32[]{:S(2)}, u32[]{:S(2)}) collective-permute-start(f32[12,320]{1,0:T(8,128)S(1)} %fusion.20), channel_id=1, source_target_pairs={{4,0},{8,4},{12,8},{16,12},{20,16},{24,20},{28,24},{5,1},{9,5},{13... | collective-permute-start | bytes 46088 | tf_op jit(solution)/shard_map/ppermute | solution.py:35
  14.6 0.3 fusion.19
  14.9 1.3 collective-permute-start.2
  16.4 0.3 fusion.18
  16.7 4.0 %collective-permute-start.3 = (f32[6,320]{1,0:T(8,128)S(1)}, f32[6,320]{1,0:T(8,128)S(1)}, u32[]{:S(2)}, u32[]{:S(2)}) collective-permute-start(f32[6,320]{1,0:T(8,128)S(1)} %fusion.18), channel_id=1, source_target_pairs={{1,0},{2,1},{3,2},{5,4},{6,5},{7,6},{9,8},{10,9},{11,10},{13,12},{... | collective-permute-start | bytes 23048 | tf_op jit(solution)/shard_map/ppermute | solution.py:35
  20.8 0.3 fusion.21
  21.1 4.4 %collective-permute-start = (f32[12,320]{1,0:T(8,128)S(1)}, f32[12,320]{1,0:T(8,128)S(1)}, u32[]{:S(2)}, u32[]{:S(2)}) collective-permute-start(f32[12,320]{1,0:T(8,128)S(1)} %fusion.21), channel_id=1, source_target_pairs={{0,4},{4,8},{8,12},{12,16},{16,20},{20,24},{24,28},{1,5},{5,9},{9,... | collective-permute-start | bytes 46088 | tf_op jit(solution)/shard_map/ppermute | solution.py:35
  26.3 0.2 convolution_bitcast_fusion.1
  26.6 0.2 fusion.52
  27.0 0.2 fusion.44
  27.2 0.2 fusion.13
  27.4 7.5 %fusion.31 = bf16[12,1,320]{2,1,0:T(2,128)(2,1)S(1)} fusion(f32[12,320,320]{2,1,0:T(8,128)} %param.14, f32[12,320,1]{1,0,2:T(8,128)S(1)} %fusion.13), kind=kOutput, calls=%fused_computation.55 | convolution fusion | flops 14745600 | bytes 4938240 | tf_op jit(solution)/shard_map/eij,ej->ei/dot_general | solution.py:121
  35.0 8.6 %fusion = f32[12,1,6,320]{3,1,2,0:T(1,128)S(1)} fusion(bf16[6,12,320,320]{3,2,1,0:T(8,128)(2,1)} %param.13, bf16[12,320,1,1]{1,0,2,3:T(8,128)(2,1)S(1)} %bitcast.150), kind=kOutput, calls=%fused_computation.2 | convolution fusion | flops 14745600 | bytes 14845440 | tf_op jit(solution)/shard_map/keij,ei->kej/dot_general | solution.py:109
  43.6 0.3 fusion.16
  43.9 0.3 fusion.15
  44.2 0.3 fusion.17
  44.4 0.3 fusion.14
  44.7 1.3 collective-permute-start.6
  46.0 0.2 convolution_bitcast_fusion
  46.2 1.9 %collective-permute-start.5 = (f32[12,320]{1,0:T(8,128)S(1)}, f32[12,320]{1,0:T(8,128)S(1)}, u32[]{:S(2)}, u32[]{:S(2)}) collective-permute-start(f32[12,320]{1,0:T(8,128)S(1)} %fusion.16), channel_id=1, source_target_pairs={{4,0},{8,4},{12,8},{16,12},{20,16},{24,20},{28,24},{5,1},{9,5},{13... | collective-permute-start | bytes 46088 | tf_op jit(solution)/shard_map/ppermute | solution.py:35
  48.2 4.5 %collective-permute-start.4 = (f32[12,320]{1,0:T(8,128)S(1)}, f32[12,320]{1,0:T(8,128)S(1)}, u32[]{:S(2)}, u32[]{:S(2)}) collective-permute-start(f32[12,320]{1,0:T(8,128)S(1)} %fusion.17), channel_id=1, source_target_pairs={{0,4},{4,8},{8,12},{12,16},{16,20},{20,24},{24,28},{1,5},{5,9},{9,... | collective-permute-start | bytes 46088 | tf_op jit(solution)/shard_map/ppermute | solution.py:35
  52.7 4.3 %collective-permute-start.7 = (f32[6,320]{1,0:T(8,128)S(1)}, f32[6,320]{1,0:T(8,128)S(1)}, u32[]{:S(2)}, u32[]{:S(2)}) collective-permute-start(f32[6,320]{1,0:T(8,128)S(1)} %fusion.14), channel_id=1, source_target_pairs={{1,0},{2,1},{3,2},{5,4},{6,5},{7,6},{9,8},{10,9},{11,10},{13,12},{... | collective-permute-start | bytes 23048 | tf_op jit(solution)/shard_map/ppermute | solution.py:35
  57.2 0.4 collective-permute-done.7
  58.0 0.2 fusion.8
  58.3 5.2 %fusion.28 = f32[12,1,320]{2,1,0:T(1,128)S(1)} fusion(f32[12,320,320]{2,1,0:T(8,128)S(1)} %bitcast.147, f32[12,320,1]{1,0,2:T(8,128)S(1)} %fusion.8), kind=kOutput, calls=%fused_computation.52 | convolution fusion | flops 14745600 | bytes 4945920 | tf_op jit(solution)/shard_map/eij,ej->ei/dot_general | solution.py:121
  63.5 0.6 convert_bitcast_fusion
  64.6 1.8 %collective-permute-start.8 = (f32[1,3,96]{2,1,0:T(4,128)S(1)}, f32[1,3,96]{2,1,0:T(4,128)S(1)}, u32[]{:S(2)}, u32[]{:S(2)}) collective-permute-start(f32[1,3,96]{2,1,0:T(4,128)S(1)} %broadcast_in_dim_reshape.3), channel_id=1, source_target_pairs={{0,1},{1,0},{2,3},{3,2},{4,5},{5,4},{6,7},{7,6},{8,9},{9,8},{10,11... | collective-permute-start | bytes 3464 | tf_op jit(solution)/shard_map/ppermute | solution.py:25
  66.5 0.9 collective-permute-done.8
  67.4 1.4 collective-permute-start.9
  69.0 1.8 %collective-permute-done.9 = f32[2,3,96]{2,1,0:T(4,128)S(1)} collective-permute-done((f32[2,3,96]{2,1,0:T(4,128)S(1)}, f32[2,3,96]{2,1,0:T(4,128)S(1)}, u32[]{:S(2)}, u32[]{:S(2)}) %collective-permute-start.9) | collective-permute-done | bytes 2336 | tf_op jit(solution)/shard_map/ppermute | solution.py:25
  70.8 1.0 collective-permute-start.10
  71.9 0.8 collective-permute-done.10
  72.8 1.0 gather_fusion
  73.8 0.3 dynamic-update-slice
  74.1 41.3 %all-reduce = s32[3072]{0:T(1024)S(1)} all-reduce(s32[3072]{0:T(1024)S(1)} %dynamic-update-slice), channel_id=2, replica_groups=mesh['dom'=8,'sub'=4] {'dom','sub'}, use_global_device_ids=true, to_apply=%add | all-reduce | flops 3072 | bytes 24576
  115.4 1.6 %collective-permute-start.12 = (f32[16,3,96]{2,0,1:T(8,128)S(1)}, f32[16,3,96]{2,0,1:T(8,128)S(1)}, u32[]{:S(2)}, u32[]{:S(2)}) collective-permute-start(f32[16,3,96]{2,0,1:T(8,128)S(1)} %get-tuple-element.13), channel_id=1, source_target_pairs={{0,16},{1,17},{2,18},{3,19},{4,20},{5,21},{6,22},{7,23},{8,24},{9,... | collective-permute-start | bytes 55304 | tf_op jit(solution)/shard_map/ppermute | solution.py:25
  117.1 1.2 collective-permute-done.12
  118.3 0.5 copy.78
  118.8 21.1 %scatter_custom_fusion = f32[19,3]{1,0:T(8,128)S(1)} fusion(s32[3072]{0:T(1024)S(1)} %and_select_fusion, f32[3072,3]{1,0:T(8,128)S(1)} %bitcast.148, f32[]{:T(128)} %constant.37.clone.1), kind=kCustom, calls=%fused_computation.95 | custom fusion | flops 9216 | bytes 232 | tf_op jit(solution)/shard_map/scatter-add | solution.py:134
  140.3 7.8 %collective-permute-start.13 = (f32[6,1]{1,0:T(8,128)S(1)}, f32[6,1]{1,0:T(8,128)S(1)}, u32[]{:S(2)}, u32[]{:S(2)}) collective-permute-start(f32[6,1]{1,0:T(8,128)S(1)} %get-tuple-element.18), channel_id=1, source_target_pairs={{0,1},{1,2},{2,3},{3,4},{4,5},{5,6},{6,7},{7,8},{8,9},{9,10},{10,1... | collective-permute-start | bytes 80 | tf_op jit(solution)/shard_map/ppermute | solution.py:43
  148.1 1.9 %collective-permute-start.14 = (f32[6,1]{1,0:T(8,128)S(1)}, f32[6,1]{1,0:T(8,128)S(1)}, u32[]{:S(2)}, u32[]{:S(2)}) collective-permute-start(f32[6,1]{1,0:T(8,128)S(1)} %get-tuple-element.19), channel_id=1, source_target_pairs={{1,0},{2,1},{3,2},{4,3},{5,4},{6,5},{7,6},{8,7},{9,8},{10,9},{11,1... | collective-permute-start | bytes 80 | tf_op jit(solution)/shard_map/ppermute | solution.py:46
  150.0 6.6 %collective-permute-done.14 = f32[6,1]{1,0:T(8,128)S(1)} collective-permute-done((f32[6,1]{1,0:T(8,128)S(1)}, f32[6,1]{1,0:T(8,128)S(1)}, u32[]{:S(2)}, u32[]{:S(2)}) %collective-permute-start.14) | collective-permute-done | bytes 56 | tf_op jit(solution)/shard_map/ppermute | solution.py:46
  156.8 0.6 bitcast_add_fusion
  (86 shorter events, 3.8 us)
Async XLA Ops:
  0.6 63.5 %copy-start = (bf16[12,24,320]{2,1,0:T(8,128)(2,1)S(1)}, bf16[12,24,320]{2,1,0:T(8,128)(2,1)}, u32[]{:S(2)}) copy-start(bf16[12,24,320]{2,1,0:T(8,128)(2,1)} %param.15) | copy-start | bytes 552964
  2.9 22.6 %copy-start.3 = (s32[12,6]{0,1:T(8,128)S(1)}, s32[12,6]{0,1:T(8,128)}, u32[]{:S(2)}) copy-start(s32[12,6]{0,1:T(8,128)} %param.16) | copy-start | bytes 868
  2.9 24.3 %copy-start.2 = (f32[12,320]{1,0:T(8,128)S(1)}, f32[12,320]{1,0:T(8,128)}, u32[]{:S(2)}) copy-start(f32[12,320]{1,0:T(8,128)} %param.11) | copy-start | bytes 46084
  11.9 15.1 %collective-permute-start.1 = (f32[12,320]{1,0:T(8,128)S(1)}, f32[12,320]{1,0:T(8,128)S(1)}, u32[]{:S(2)}, u32[]{:S(2)}) collective-permute-start(f32[12,320]{1,0:T(8,128)S(1)} %fusion.20), channel_id=1, source_target_pairs={{4,0},{8,4},{12,8},{16,12},{20,16},{24,20},{28,24},{5,1},{9,5},{13... | collective-permute-start | bytes 46088 | tf_op jit(solution)/shard_map/ppermute | solution.py:35
  14.9 11.7 %collective-permute-start.2 = (f32[6,320]{1,0:T(8,128)S(1)}, f32[6,320]{1,0:T(8,128)S(1)}, u32[]{:S(2)}, u32[]{:S(2)}) collective-permute-start(f32[6,320]{1,0:T(8,128)S(1)} %fusion.19), channel_id=1, source_target_pairs={{0,1},{1,2},{2,3},{4,5},{5,6},{6,7},{8,9},{9,10},{10,11},{12,13},{... | collective-permute-start | bytes 23048 | tf_op jit(solution)/shard_map/ppermute | solution.py:35
  16.7 10.1 %collective-permute-start.3 = (f32[6,320]{1,0:T(8,128)S(1)}, f32[6,320]{1,0:T(8,128)S(1)}, u32[]{:S(2)}, u32[]{:S(2)}) collective-permute-start(f32[6,320]{1,0:T(8,128)S(1)} %fusion.18), channel_id=1, source_target_pairs={{1,0},{2,1},{3,2},{5,4},{6,5},{7,6},{9,8},{10,9},{11,10},{13,12},{... | collective-permute-start | bytes 23048 | tf_op jit(solution)/shard_map/ppermute | solution.py:35
  21.1 6.1 %collective-permute-start = (f32[12,320]{1,0:T(8,128)S(1)}, f32[12,320]{1,0:T(8,128)S(1)}, u32[]{:S(2)}, u32[]{:S(2)}) collective-permute-start(f32[12,320]{1,0:T(8,128)S(1)} %fusion.21), channel_id=1, source_target_pairs={{0,4},{4,8},{8,12},{12,16},{16,20},{20,24},{24,28},{1,5},{5,9},{9,... | collective-permute-start | bytes 46088 | tf_op jit(solution)/shard_map/ppermute | solution.py:35
  27.4 30.8 %slice-start = ((s8[5898240]{0:T(1024)(128)(4,1)}), s8[4194304]{0:T(1024)(128)(4,1)S(1)}, s32[]{:S(2)}) async-start(s8[5898240]{0:T(1024)(128)(4,1)} %bitcast.146), calls=%async_computation | async-start | bytes 8388608
  35.0 23.3 %slice-start.1 = ((s8[5898240]{0:T(1024)(128)(4,1)}), s8[1703936]{0:T(1024)(128)(4,1)S(1)}, s32[]{:S(2)}) async-start(s8[5898240]{0:T(1024)(128)(4,1)} %bitcast.146), calls=%async_computation.1 | async-start | bytes 3407872
  43.6 25.2 %copy-start.7 = (s32[12,8]{0,1:T(8,128)S(1)}, s32[12,8]{0,1:T(8,128)}, u32[]{:S(2)}) copy-start(s32[12,8]{0,1:T(8,128)} %param.17) | copy-start | bytes 1156
  43.6 29.2 %copy-start.1 = (s32[567]{0:T(1024)S(1)}, s32[567]{0:T(1024)}, u32[]{:S(2)}) copy-start(s32[567]{0:T(1024)} %param.18) | copy-start | bytes 6808
  43.6 96.6 %copy-start.5 = (f32[3,3,18]{2,1,0:T(4,128)S(1)}, f32[3,3,18]{2,1,0:T(4,128)}, u32[]{:S(2)}) copy-start(f32[3,3,18]{2,1,0:T(4,128)} %param.19) | copy-start | bytes 1948
  43.6 96.6 %copy-start.6 = (f32[3,3,18]{2,1,0:T(4,128)S(1)}, f32[3,3,18]{2,1,0:T(4,128)}, u32[]{:S(2)}) copy-start(f32[3,3,18]{2,1,0:T(4,128)} %param.20) | copy-start | bytes 1948
  43.6 113.1 %copy-start.4 = (f32[3,3,18]{2,1,0:T(4,128)S(1)}, f32[3,3,18]{2,1,0:T(4,128)}, u32[]{:S(2)}) copy-start(f32[3,3,18]{2,1,0:T(4,128)} %param.21) | copy-start | bytes 1948
  44.7 12.3 %collective-permute-start.6 = (f32[6,320]{1,0:T(8,128)S(1)}, f32[6,320]{1,0:T(8,128)S(1)}, u32[]{:S(2)}, u32[]{:S(2)}) collective-permute-start(f32[6,320]{1,0:T(8,128)S(1)} %fusion.15), channel_id=1, source_target_pairs={{0,1},{1,2},{2,3},{4,5},{5,6},{6,7},{8,9},{9,10},{10,11},{12,13},{... | collective-permute-start | bytes 23048 | tf_op jit(solution)/shard_map/ppermute | solution.py:35
  46.2 11.6 %collective-permute-start.5 = (f32[12,320]{1,0:T(8,128)S(1)}, f32[12,320]{1,0:T(8,128)S(1)}, u32[]{:S(2)}, u32[]{:S(2)}) collective-permute-start(f32[12,320]{1,0:T(8,128)S(1)} %fusion.16), channel_id=1, source_target_pairs={{4,0},{8,4},{12,8},{16,12},{20,16},{24,20},{28,24},{5,1},{9,5},{13... | collective-permute-start | bytes 46088 | tf_op jit(solution)/shard_map/ppermute | solution.py:35
  48.2 9.9 %collective-permute-start.4 = (f32[12,320]{1,0:T(8,128)S(1)}, f32[12,320]{1,0:T(8,128)S(1)}, u32[]{:S(2)}, u32[]{:S(2)}) collective-permute-start(f32[12,320]{1,0:T(8,128)S(1)} %fusion.17), channel_id=1, source_target_pairs={{0,4},{4,8},{8,12},{12,16},{16,20},{20,24},{24,28},{1,5},{5,9},{9,... | collective-permute-start | bytes 46088 | tf_op jit(solution)/shard_map/ppermute | solution.py:35
  52.7 4.9 %collective-permute-start.7 = (f32[6,320]{1,0:T(8,128)S(1)}, f32[6,320]{1,0:T(8,128)S(1)}, u32[]{:S(2)}, u32[]{:S(2)}) collective-permute-start(f32[6,320]{1,0:T(8,128)S(1)} %fusion.14), channel_id=1, source_target_pairs={{1,0},{2,1},{3,2},{5,4},{6,5},{7,6},{9,8},{10,9},{11,10},{13,12},{... | collective-permute-start | bytes 23048 | tf_op jit(solution)/shard_map/ppermute | solution.py:35
  64.6 2.8 %collective-permute-start.8 = (f32[1,3,96]{2,1,0:T(4,128)S(1)}, f32[1,3,96]{2,1,0:T(4,128)S(1)}, u32[]{:S(2)}, u32[]{:S(2)}) collective-permute-start(f32[1,3,96]{2,1,0:T(4,128)S(1)} %broadcast_in_dim_reshape.3), channel_id=1, source_target_pairs={{0,1},{1,0},{2,3},{3,2},{4,5},{5,4},{6,7},{7,6},{8,9},{9,8},{10,11... | collective-permute-start | bytes 3464 | tf_op jit(solution)/shard_map/ppermute | solution.py:25
  67.4 3.4 %collective-permute-start.9 = (f32[2,3,96]{2,1,0:T(4,128)S(1)}, f32[2,3,96]{2,1,0:T(4,128)S(1)}, u32[]{:S(2)}, u32[]{:S(2)}) collective-permute-start(f32[2,3,96]{2,1,0:T(4,128)S(1)} %get-tuple-element.21), channel_id=1, source_target_pairs={{0,2},{1,3},{2,0},{3,1},{4,6},{5,7},{6,4},{7,5},{8,10},{9,11},{10,... | collective-permute-start | bytes 6920 | tf_op jit(solution)/shard_map/ppermute | solution.py:25
  70.8 1.8 %collective-permute-start.10 = (f32[4,3,96]{2,1,0:T(4,128)S(1)}, f32[4,3,96]{2,1,0:T(4,128)S(1)}, u32[]{:S(2)}, u32[]{:S(2)}) collective-permute-start(f32[4,3,96]{2,1,0:T(4,128)S(1)} %bitcast.163), channel_id=1, source_target_pairs={{0,4},{1,5},{2,6},{3,7},{4,0},{5,1},{6,2},{7,3},{8,12},{9,13},{10,... | collective-permute-start | bytes 13832 | tf_op jit(solution)/shard_map/ppermute | solution.py:25
  72.7 42.7 %collective-permute-start.11 = (f32[8,3,96]{2,0,1:T(8,128)S(1)}, f32[8,3,96]{2,0,1:T(8,128)S(1)}, u32[]{:S(2)}, u32[]{:S(2)}) collective-permute-start(f32[8,3,96]{2,0,1:T(8,128)S(1)} %copy.41), channel_id=1, source_target_pairs={{0,8},{1,9},{2,10},{3,11},{4,12},{5,13},{6,14},{7,15},{8,0},{9,1},... | collective-permute-start | bytes 27656 | tf_op jit(solution)/shard_map/ppermute | solution.py:25
  115.4 2.9 %collective-permute-start.12 = (f32[16,3,96]{2,0,1:T(8,128)S(1)}, f32[16,3,96]{2,0,1:T(8,128)S(1)}, u32[]{:S(2)}, u32[]{:S(2)}) collective-permute-start(f32[16,3,96]{2,0,1:T(8,128)S(1)} %get-tuple-element.13), channel_id=1, source_target_pairs={{0,16},{1,17},{2,18},{3,19},{4,20},{5,21},{6,22},{7,23},{8,24},{9,... | collective-permute-start | bytes 55304 | tf_op jit(solution)/shard_map/ppermute | solution.py:25
  140.3 9.7 %collective-permute-start.13 = (f32[6,1]{1,0:T(8,128)S(1)}, f32[6,1]{1,0:T(8,128)S(1)}, u32[]{:S(2)}, u32[]{:S(2)}) collective-permute-start(f32[6,1]{1,0:T(8,128)S(1)} %get-tuple-element.18), channel_id=1, source_target_pairs={{0,1},{1,2},{2,3},{3,4},{4,5},{5,6},{6,7},{7,8},{8,9},{9,10},{10,1... | collective-permute-start | bytes 80 | tf_op jit(solution)/shard_map/ppermute | solution.py:43
  148.1 8.5 %collective-permute-start.14 = (f32[6,1]{1,0:T(8,128)S(1)}, f32[6,1]{1,0:T(8,128)S(1)}, u32[]{:S(2)}, u32[]{:S(2)}) collective-permute-start(f32[6,1]{1,0:T(8,128)S(1)} %get-tuple-element.19), channel_id=1, source_target_pairs={{1,0},{2,1},{3,2},{4,3},{5,4},{6,5},{7,6},{8,7},{9,8},{10,9},{11,1... | collective-permute-start | bytes 80 | tf_op jit(solution)/shard_map/ppermute | solution.py:46
